TPU v7x, 256 devices: a whole 4x4x8 slice. The times are simulated.
256 devices in a mesh: seq: 64 (over z, y, core), mp: 4 (over x).
Axes of the slice: x: 4, y: 4, z: 8, core: 2. Of those that a mesh axis runs over, the one named last changes fastest.
Arguments:
- queries: bfloat16 [131072, 4096], P('seq', 'mp'), may hold values from -1000 to 1000, as said below
- encoded: bfloat16 [256, 32, 896], P('seq'), may hold values from -6 to 6
- w_kv: bfloat16 [896, 2, 4096], P(None, None, 'mp'), may hold values from -0.1875 to 0.1875
- retrieved: int32 [2048, 2], P('seq'), may hold values from 0 to 255, as said below
Outputs:
- attended: bfloat16 [131072, 4096], P('seq', 'mp')
Inputs may be any that keep to these rules, and one draw needn't show every extreme that they name: Decoder queries; their rows have unequal scales. `retrieved`: tile i is stored on index i // 4 of seq; of the 64 ids of one index of seq, exactly 1 name tiles stored on each index of seq; a tile may be named by many groups.
All inputs are finite; a program needn't handle non-finite values.
Results may differ from a plain program's by a relative error of at most 0.012.
Values may be sent and summed in bfloat16 or wider, within the bound.
A program may use at most 128 MiB of HBM per device.

v0:
```python
import jax
import jax.numpy as jnp
from jax import lax
from jax.sharding import PartitionSpec as P

GROUP = 64
HEAD_DIM = 128


def project_rows(tiles, weights):
    count, rows, width = tiles.shape
    flat = jnp.dot(tiles.reshape(count * rows, width), weights, preferred_element_type=jnp.float32)
    return flat.astype(jnp.bfloat16).reshape(count, rows, weights.shape[1])


def ref_ranks(owners):
    length = owners.shape[-1]
    position = jnp.arange(length)
    earlier = position[None, :] < position[:, None]
    same_owner = owners[..., :, None] == owners[..., None, :]
    return jnp.sum(same_owner & earlier, axis=-1)


def body(queries, encoded, w_kv, retrieved):
    seq_count = lax.axis_size("seq")
    group_count = retrieved.shape[0]
    ref_count = 2 * group_count
    tile_count = encoded.shape[0]
    capacity = (ref_count + seq_count - 1) // seq_count
    slot_count = seq_count * capacity
    tile_ids = retrieved.reshape(ref_count)
    owners = tile_ids // tile_count
    slot_ids = owners * capacity + ref_ranks(owners)
    wanted = jnp.arange(slot_count, dtype=jnp.int32)[:, None] == slot_ids[None, :]
    request = jnp.sum(jnp.where(wanted, (tile_ids % tile_count)[None, :], 0), axis=1)
    asked = lax.all_to_all(request, "seq", split_axis=0, concat_axis=0, tiled=True)
    outgoing = jnp.take(encoded, asked, axis=0)
    weights = w_kv.reshape(w_kv.shape[0], -1)
    key_value = project_rows(
        jnp.take(
            lax.all_to_all(outgoing, "seq", split_axis=0, concat_axis=0, tiled=True),
            slot_ids,
            axis=0,
        ),
        weights,
    )
    local_width = queries.shape[1]
    heads_here = local_width // HEAD_DIM
    paired = key_value.reshape(group_count, 2 * key_value.shape[1], 2, heads_here, HEAD_DIM)
    key_rows = paired[:, :, 0]
    value_rows = paired[:, :, 1]
    query_heads = queries.reshape(group_count, GROUP, heads_here, HEAD_DIM)
    scores = jnp.einsum(
        "cthe,cshe->chts", query_heads, key_rows, preferred_element_type=jnp.float32
    ) * HEAD_DIM ** (-0.5)
    top = jnp.max(scores, axis=-1, keepdims=True)
    expd = jnp.exp(scores - top)
    probs = (expd / jnp.sum(expd, axis=-1, keepdims=True)).astype(jnp.bfloat16)
    mixed = jnp.einsum("chts,cshe->cthe", probs, value_rows, preferred_element_type=jnp.float32)
    return mixed.astype(jnp.bfloat16).reshape(group_count * GROUP, local_width)


def solution(mesh):
    in_specs = (P("seq", "mp"), P("seq", None, None), P(None, None, "mp"), P("seq", None))
    out_specs = P("seq", "mp")
    return jax.shard_map(body, mesh=mesh, in_specs=in_specs, out_specs=out_specs, check_vma=False)
```

profile of v0, /device:TPU:1, one launch (start us, length us, event | category | flops | bytes accessed | tf_op | source)
XLA Modules:
  0.0 178.1 jit_solution(8934774969053284724)
XLA Ops:
  0.0 0.8 copy.34
  0.8 0.1 reshape.248
  0.9 0.2 convert_reduce_fusion
  1.1 0.1 select_reduce_fusion
  1.3 22.3 %all_to_all.20 = s32[64,1,1]{2,1,0:T(1,128)S(1)} all-to-all(s32[64,1,1]{2,1,0:T(1,128)S(1)} %copy.35), channel_id=1, replica_groups=mesh['seq'=64,'mp'=4] {'seq'}, dimensions={0} | all-to-all | bytes 512 | tf_op jit(solution)/shard_map/all_to_all | solution.py:36
  23.7 1.2 reduce
  24.9 2.8 %gather_fusion = bf16[64,32,896]{2,1,0:T(8,128)(2,1)} fusion(bf16[4,32,896]{2,1,0:T(8,128)(2,1)S(1)} %copy-done, s32[1024]{0:T(1024)S(1)} %pad_clamp_fusion.1), kind=kCustom, calls=%fused_computation | custom fusion | bytes 7340288 | tf_op jit(solution)/shard_map/jit(_take)/gather | solution.py:37
  27.7 4.4 %broadcast_select_fusion = bf16[64,32,896]{2,1,0:T(8,128)(2,1)} fusion(bf16[64,32,896]{2,1,0:T(8,128)(2,1)} %gather_fusion, pred[64]{0:T(512)(128)(4,1)S(1)} %compare_and_fusion), kind=kLoop, calls=%fused_computation.19 | loop fusion | flops 1835008 | bytes 7340096 | tf_op jit(solution)/shard_map/jit(_take)/select_n | solution.py:37
  32.1 5.7 %all-to-all-start.1 = ((bf16[64,32,896]{2,1,0:T(8,128)(2,1)}), bf16[64,32,896]{2,1,0:T(8,128)(2,1)}, u32[]{:S(2)}, u32[]{:S(2)}) async-start(bf16[64,32,896]{2,1,0:T(8,128)(2,1)} %broadcast_select_fusion), calls=%async_computation.1 | async-start | bytes 7340032 | tf_op jit(solution)/shard_map/all_to_all | solution.py:41
  37.9 5.2 %copy.45 = bf16[112,8,2,1024]{3,1,2,0:T(8,128)(2,1)} copy(bf16[112,8,2,1024]{3,2,1,0:T(2,128)(2,1)} %bitcast.53) | data formatting | bytes 7340032
  43.1 3.1 %copy.47 = bf16[256,8,8,128]{3,2,1,0:T(8,128)(2,1)} copy(bf16[256,8,8,128]{3,1,2,0:T(8,128)(2,1)S(1)} %bitcast.52) | data formatting | bytes 8388608
  46.3 75.4 %all-to-all-done.1 = bf16[64,32,896]{2,1,0:T(8,128)(2,1)} async-done(((bf16[64,32,896]{2,1,0:T(8,128)(2,1)}), bf16[64,32,896]{2,1,0:T(8,128)(2,1)}, u32[]{:S(2)}, u32[]{:S(2)}) %all-to-all-start.1) | async-done | bytes 3670048 | tf_op jit(solution)/shard_map/all_to_all | solution.py:41
  121.6 4.9 %gather_fusion.1 = bf16[64,32,896]{2,1,0:T(8,128)(2,1)} fusion(bf16[64,32,896]{2,1,0:T(8,128)(2,1)} %all-to-all-done.1, s32[1024]{0:T(1024)S(1)} %pad_clamp_fusion), kind=kCustom, calls=%fused_computation.1 | custom fusion | bytes 7340288 | tf_op jit(solution)/shard_map/jit(_take)/gather | solution.py:40
  126.5 2.6 %broadcast_select_fusion.1 = bf16[64,32,896]{2,1,0:T(8,128)(2,1)S(1)} fusion(bf16[64,32,896]{2,1,0:T(8,128)(2,1)} %gather_fusion.1, pred[64]{0:T(512)(128)(4,1)S(1)} %get-tuple-element.5), kind=kLoop, calls=%fused_computation.20 | loop fusion | flops 1835008 | bytes 7340096 | tf_op jit(solution)/shard_map/jit(_take)/select_n | solution.py:40
  129.2 0.5 copy-done.4
  129.7 10.9 %convert_bitcast_fusion = bf16[256,8,16,128]{3,1,2,0:T(8,128)(2,1)} fusion(bf16[2048,896]{1,0:T(8,128)(2,1)S(1)} %bitcast.55, bf16[896,2048]{1,0:T(8,128)(2,1)S(1)} %bitcast.54), kind=kOutput, calls=%fused_computation.8 | convolution fusion | flops 7520387072 | bytes 15728640 | tf_op jit(solution)/shard_map/dot_general | solution.py:12
  140.5 9.7 %copy.46 = bf16[256,8,16,128]{3,2,1,0:T(8,128)(2,1)} copy(bf16[256,8,16,128]{3,1,2,0:T(8,128)(2,1)} %convert_bitcast_fusion) | data formatting | bytes 16777216
  150.3 4.0 %fusion.15 = (bf16[32,64,1,8,128]{4,3,2,1,0:T(8,128)(2,1)S(1)}, bf16[32,64,1,8,128]{4,3,2,1,0:T(8,128)(2,1)S(1)}) fusion(bf16[32,64,2,8,128]{4,3,2,1,0:T(8,128)(2,1)} %bitcast.49), kind=kLoop, calls=%fused_computation.47 | loop fusion | bytes 16777216 | tf_op jit(solution)/shard_map/slice | solution.py:51
  154.3 0.6 copy-done.2
  154.9 2.3 %fusion.7 = f32[32,8,64,64]{3,2,1,0:T(8,128)S(1)} fusion(bf16[32,64,1,8,128]{4,3,2,1,0:T(8,128)(2,1)S(1)} %get-tuple-element.8, bf16[32,64,8,128]{3,2,1,0:T(8,128)(2,1)S(1)} %bitcast.51), kind=kOutput, calls=%fused_computation.13 | convolution fusion | flops 268435456 | bytes 12582912 | tf_op jit(solution)/shard_map/cthe,cshe->chts/dot_general | solution.py:53
  157.2 4.5 %fusion.16 = (f32[32,8,64]{2,1,0:T(8,128)S(1)}, f32[32,8,64,64]{2,3,1,0:T(8,128)}) fusion(f32[32,8,64,64]{3,2,1,0:T(8,128)S(1)} %fusion.7), kind=kOutput, calls=%fused_computation.48 | output fusion | flops 4194367 | bytes 8454144 | tf_op jit(solution)/shard_map/sub | solution.py:57
  161.7 5.0 %convert_bitcast_fusion.1 = bf16[32,64,8,128]{3,1,2,0:T(8,128)(2,1)S(1)} fusion(f32[32,8,64,64]{2,3,1,0:T(8,128)} %get-tuple-element.12, f32[32,8,64]{2,1,0:T(8,128)S(1)} %get-tuple-element.11, bf16[32,64,1,8,128]{4,3,2,1,0:T(8,128)(2,1)S(1)} %get-tuple-element.7), kind=kOutput, calls=%fused_computation.16 | convolution fusion | flops 272629760 | bytes 12648448 | tf_op jit(solution)/shard_map/chts,cshe->cthe/dot_general | solution.py:59
  166.8 8.1 %copy.41 = bf16[32,64,8,128]{3,2,1,0:T(8,128)(2,1)S(1)} copy(bf16[32,64,8,128]{3,1,2,0:T(8,128)(2,1)S(1)} %convert_bitcast_fusion.1) | data formatting | bytes 8388608 | tf_op jit(solution)/shard_map/convert_element_type | solution.py:60
  175.0 3.1 %copy.58 = bf16[256,8,8,128]{3,1,2,0:T(8,128)(2,1)} copy(bf16[256,8,8,128]{3,2,1,0:T(8,128)(2,1)S(1)} %bitcast.50) | data formatting | bytes 8388608
  (17 shorter events, 0.3 us)
Async XLA Ops:
  0.0 24.9 %copy-start = (bf16[4,32,896]{2,1,0:T(8,128)(2,1)S(1)}, bf16[4,32,896]{2,1,0:T(8,128)(2,1)}, u32[]{:S(2)}) copy-start(bf16[4,32,896]{2,1,0:T(8,128)(2,1)} %param.5) | copy-start | bytes 688132
  32.1 89.5 %all-to-all-start.1 = ((bf16[64,32,896]{2,1,0:T(8,128)(2,1)}), bf16[64,32,896]{2,1,0:T(8,128)(2,1)}, u32[]{:S(2)}, u32[]{:S(2)}) async-start(bf16[64,32,896]{2,1,0:T(8,128)(2,1)} %broadcast_select_fusion), calls=%async_computation.1 | async-start | bytes 7340032 | tf_op jit(solution)/shard_map/all_to_all | solution.py:41
  37.9 5.3 %copy-start.3 = (bf16[2048,1024]{1,0:T(8,128)(2,1)S(1)}, bf16[2048,1024]{1,0:T(8,128)(2,1)}, u32[]{:S(2)}) copy-start(bf16[2048,1024]{1,0:T(8,128)(2,1)} %param.4) | copy-start | bytes 12582916
  126.5 3.1 %copy-start.4 = (bf16[112,8,2,1024]{3,1,2,0:T(8,128)(2,1)S(1)}, bf16[112,8,2,1024]{3,1,2,0:T(8,128)(2,1)}, u32[]{:S(2)}) copy-start(bf16[112,8,2,1024]{3,1,2,0:T(8,128)(2,1)} %copy.45) | copy-start | bytes 11010052
  150.3 4.7 %copy-start.2 = (bf16[256,8,8,128]{3,2,1,0:T(8,128)(2,1)S(1)}, bf16[256,8,8,128]{3,2,1,0:T(8,128)(2,1)}, u32[]{:S(2)}) copy-start(bf16[256,8,8,128]{3,2,1,0:T(8,128)(2,1)} %copy.47) | copy-start | bytes 12582916
  174.9 3.1 %copy-start.1 = (bf16[4,32,896]{2,1,0:T(8,128)(2,1)S(1)}, bf16[4,32,896]{2,1,0:T(8,128)(2,1)}, u32[]{:S(2)}) copy-start(bf16[4,32,896]{2,1,0:T(8,128)(2,1)} %param.5) | copy-start | bytes 688132
where the time goes:
time: 179 us; the launch traced here: 178 us
  waiting for transfers between devices  75.4 us (42%)
  local copies, waits for them, and re-layouts  43.3 us (24%)
  blocking collectives  22.3 us (12%)
  matrix products  18.2 us (10%)
  other arithmetic  13.1 us (7%)
  starting transfers between devices  5.66 us (3%)
    all_to_all x1, waiting for transfers between devices, body(): lax.all_to_all(outgoing, 'seq', split_axis=0, concat_axis=0, tiled=True)  75.4 us
    unnamed x15, local copies, waits for them, and re-layouts  23.2 us
    all_to_all x1, blocking collectives, body(): lax.all_to_all(request, 'seq', split_axis=0, concat_axis=0, tiled=True)  22.3 us
    dot_general x1, matrix products, project_rows(): jnp.dot(tiles.reshape(count * rows, width), weights, preferred_element_ty...  10.9 us
    convert_element_type x1, local copies, waits for them, and re-layouts, body(): return mixed.astype(jnp.bfloat16).reshape(group_count * GROUP, local_width)  8.14 us
    all_to_all x1, starting transfers between devices, body(): lax.all_to_all(outgoing, 'seq', split_axis=0, concat_axis=0, tiled=True)  5.66 us
    dot_general x1, matrix products, body(): jnp.einsum('chts,cshe->cthe', probs, value_rows, preferred_element_type=j...  5.05 us
    gather x1, local copies, waits for them, and re-layouts, body(): jnp.take(lax.all_to_all(outgoing, 'seq', split_axis=0, concat_axis=0, til...  4.89 us
  transfers between devices with their start and end apart: 1, of which 1 were waited for; matrix products, arithmetic and copies ran while one was open for 5% of the time, Pallas kernels for 0%

commit v1 on v0

v1 whole, which is shorter than its diff:
```python
import functools

import jax
import jax.numpy as jnp
from jax import lax
from jax.experimental import pallas as pl
from jax.experimental.pallas import tpu as pltpu
from jax.sharding import PartitionSpec as P

GROUP = 64
HEAD_DIM = 128
TILES = 4
CORES = 2
MESH = pl.DeviceIdType.MESH
SCALE = (HEAD_DIM ** -0.5) * 1.4426950408889634


def step_distance(step, nz):
    return jnp.where(step % 2 == 1, (step + 1) // 2, (nz - step // 2) % nz)


def gather_kernel(nz, ny, ids_ref, enc_ref, w_ref, kv_ref,
                  ids_in, sel, pool, picked, rows, w_raw, w_flat, staged,
                  ids_send, ids_recv, z_send, z_recv, y_send, y_recv, x_send, x_recv, own_sem, w_sem, kv_sem):
    seq, x = lax.axis_index("seq"), lax.axis_index("mp")
    nx = lax.axis_size("mp")
    z, y, c = seq // (ny * CORES), (seq // CORES) % ny, seq % CORES
    half = x % 2
    nr = ny * CORES
    right, left = (seq, (x + 1) % nx), (seq, (x + nx - 1) % nx)

    def along_z(k):
        return (((z + k) % nz * ny + y) * CORES + c, x)

    def in_row(r):
        return ((z * ny + (y + r % ny) % ny) * CORES + (c + r // ny) % CORES, x)

    def in_row_back(r):
        return ((z * ny + (y + ny - r % ny) % ny) * CORES + (c + r // ny) % CORES, x)

    barrier = pltpu.get_barrier_semaphore()
    for k in range(1, nz):
        pl.semaphore_signal(barrier, inc=1, device_id=along_z(k), device_id_type=MESH)
    for r in range(1, nr):
        pl.semaphore_signal(barrier, inc=1, device_id=in_row(r), device_id_type=MESH)
    for to in (right, left):
        pl.semaphore_signal(barrier, inc=1, device_id=to, device_id_type=MESH)
    own_copy = pltpu.make_async_copy(enc_ref.at[:, half], pool.at[0], own_sem)
    own_copy.start()
    w_copy = pltpu.make_async_copy(w_ref, w_raw, w_sem)
    w_copy.start()
    pl.semaphore_wait(barrier, nz + nr)

    def ids_copy(r):
        return pltpu.make_async_remote_copy(ids_ref, ids_in.at[r], ids_send.at[r], ids_recv.at[r],
                                            device_id=in_row_back(r), device_id_type=MESH)

    def z_copy(step):
        k = step_distance(step, nz)
        return pltpu.make_async_remote_copy(enc_ref.at[:, half], pool.at[step], z_send.at[step], z_recv.at[step],
                                            device_id=along_z(k), device_id_type=MESH)

    def y_copy(step, r):
        return pltpu.make_async_remote_copy(picked.at[step, r], rows.at[step, r, half], y_send.at[step, r],
                                            y_recv.at[step, r], device_id=in_row(r), device_id_type=MESH)

    def x_copy(step, d):
        part = rows.at[step, pl.ds(d * ny, ny), half]
        return pltpu.make_async_remote_copy(part, part, x_send.at[step, d], x_recv.at[step, d],
                                            device_id=(right, left)[d], device_id_type=MESH)

    def x_arrival(step, d):
        part = rows.at[step, pl.ds(d * ny, ny), 1 - half]
        return pltpu.make_async_remote_copy(part, part, x_send.at[step, d], x_recv.at[step, d],
                                            device_id=(right, left)[d], device_id_type=MESH)

    for r in range(1, nr):
        ids_copy(r).start()
    for step in range(1, nz):
        z_copy(step).start()

    steps = lax.broadcasted_iota(jnp.int32, (nz, 1), 0)
    owner = ((z + nz - step_distance(steps, nz)) % nz * ny + y) * CORES + c
    for r in range(nr):
        if r > 0:
            ids_copy(r).wait_recv()
        ids = ids_ref[...] if r == 0 else ids_in[r]
        for t in range(TILES):
            hit = (ids[0:1] == owner * TILES + t) | (ids[1:2] == owner * TILES + t)
            count = jnp.sum(jnp.where(hit, 1.0, 0.0), axis=1, keepdims=True)
            sel[r, t] = jnp.broadcast_to(count, (nz, 128))

    def pick(step):
        width = pool.shape[-1] // 128
        tiles = [pool[step, t] for t in range(TILES)]
        for r in range(nr):
            total = None
            for t in range(TILES):
                lane = jnp.broadcast_to(sel[r, t, pl.ds(step, 1), :], (16, 128)).astype(jnp.bfloat16)
                term = tiles[t] * jnp.concatenate([lane] * width, axis=1)
                total = term if total is None else total + term
            if r == 0:
                rows[step, 0, half] = total
            else:
                picked[step, r] = total
                y_copy(step, r).start()

    own_copy.wait()
    pick(0)

    w_copy.wait()
    kinds = w_flat.shape[1] // 128
    per = 256 // kinds
    out_row = lax.broadcasted_iota(jnp.int32, (256, 256), 0)
    in_col = lax.broadcasted_iota(jnp.int32, (256, 256), 1)
    order = jnp.where(in_col == out_row % per * kinds + out_row // per, 1.0, 0.0).astype(jnp.bfloat16)

    def unweave(i, _):
        for u in range(2):
            b = i * 2 + u
            block = w_raw[pl.ds(pl.multiple_of(b * 256, 256), 256), :]
            sorted_rows = jnp.dot(order, block, preferred_element_type=jnp.float32).astype(jnp.bfloat16)
            for kind in range(kinds):
                at = (kind % 2) * (kinds // 2) + kind // 2
                w_flat[pl.ds(pl.multiple_of(b * per, per), per), at * 128:at * 128 + 128] = sorted_rows[kind * per:(kind + 1) * per]
        return 0

    lax.fori_loop(0, w_raw.shape[0] // 512, unweave, 0)

    def kv_copy(step):
        return pltpu.make_async_copy(staged.at[step % 2], kv_ref.at[pl.ds(step * nr, nr)], kv_sem.at[step % 2])

    def project(step):
        for d in range(2):
            x_arrival(step, d).wait_recv()

        @pl.when(step >= 2)
        def _():
            kv_copy(step - 2).wait()

        flat = rows[step].reshape(nr * 32, rows.shape[-1])

        def columns(i, _):
            at = pl.ds(pl.multiple_of(i * 512, 512), 512)
            part = jnp.dot(flat, w_flat[:, at], preferred_element_type=jnp.float32).astype(jnp.bfloat16)
            staged[step % 2, :, :, at] = part.reshape(nr, 32, 512)
            return 0

        lax.fori_loop(0, w_flat.shape[1] // 512, columns, 0)
        kv_copy(step).start()

    def body(i, _):
        @pl.when(i < nz)
        def _():
            z_copy(i).wait_recv()
            pick(i)

        @pl.when(i <= nz)
        def _():
            for d in range(2):
                for r in range(d * ny, (d + 1) * ny):
                    if r > 0:
                        y_copy(i - 1, r).wait_recv()
                x_copy(i - 1, d).start()

        @pl.when(i >= 2)
        def _():
            project(i - 2)

        return 0

    lax.fori_loop(1, nz + 2, body, 0)

    for step in range(nz - 2, nz):
        kv_copy(step).wait()
    for r in range(1, nr):
        ids_copy(r).wait_send()

    def drain(step, _):
        @pl.when(step > 0)
        def _():
            z_copy(step).wait_send()

        for r in range(1, nr):
            y_copy(step, r).wait_send()
        for d in range(2):
            x_copy(step, d).wait_send()
        return 0

    lax.fori_loop(0, nz, drain, 0)


def gather_and_project(ids, encoded, weights, nz, ny):
    count, rows, width = encoded.shape
    nr = ny * CORES
    features = weights.shape[0] * 128 // width
    dma = pltpu.SemaphoreType.DMA
    hbm = pl.BlockSpec(memory_space=pltpu.HBM)
    bf16 = jnp.bfloat16
    slots = nz * nr
    return pl.pallas_call(
        functools.partial(gather_kernel, nz, ny),
        out_shape=jax.ShapeDtypeStruct((slots, rows, features), bf16),
        in_specs=[pl.BlockSpec(memory_space=pltpu.VMEM), hbm, hbm],
        out_specs=hbm,
        scratch_shapes=[
            pltpu.VMEM((nr,) + ids.shape, jnp.int32),
            pltpu.VMEM((nr, TILES, nz, 128), jnp.float32),
            pltpu.VMEM((nz, TILES, 16, width), bf16),
            pltpu.VMEM((nz, nr, 16, width), bf16),
            pltpu.VMEM((nz, nr, 2, 16, width), bf16),
            pltpu.VMEM(weights.shape, bf16),
            pltpu.VMEM((width, features), bf16),
            pltpu.VMEM((2, nr, rows, features), bf16),
            dma((nr,)), dma((nr,)), dma((nz,)), dma((nz,)), dma((nz, nr)), dma((nz, nr)), dma((nz, 2)), dma((nz, 2)),
            dma, dma, dma((2,)),
        ],
        compiler_params=pltpu.CompilerParams(collective_id=0, has_side_effects=True, vmem_limit_bytes=58 << 20),
        cost_estimate=pl.CostEstimate(flops=2 * slots * rows * width * features, bytes_accessed=16 << 20, transcendentals=0),
    )(ids, encoded.reshape(count, 2, rows // 2, width), weights)


def attend_kernel(chunk, slots_ref, q_hbm, kv_hbm, o_hbm, q, kv, o, q_sem, kv_sem, o_sem):
    groups = q.shape[0] // GROUP
    chunks = groups // chunk
    width = q.shape[1]
    span = chunk * GROUP

    def q_copy(i):
        at = pl.ds(i * span, span)
        return pltpu.make_async_copy(q_hbm.at[at], q.at[at], q_sem.at[i])

    def o_copy(i):
        at = pl.ds(i * span, span)
        return pltpu.make_async_copy(o.at[at], o_hbm.at[at], o_sem.at[i])

    for i in range(chunks):
        q_copy(i).start()
        for j in range(2 * chunk * i, 2 * chunk * (i + 1)):
            pltpu.make_async_copy(kv_hbm.at[slots_ref[j]], kv.at[j], kv_sem.at[i]).start()

    zero = jnp.zeros((GROUP, HEAD_DIM), jnp.bfloat16)

    def step(i, _):
        q_copy(i).wait()
        part = kv.at[pl.ds(i * 2 * chunk, 2 * chunk)]
        pltpu.make_async_copy(part, part, kv_sem.at[i]).wait()
        for u in range(chunk):
            g = i * chunk + u
            row = pl.ds(pl.multiple_of(g * GROUP, GROUP), GROUP)
            both = pl.ds(2 * g, 2)
            for h in range(width // 256):
                at = slice(h * 256, h * 256 + 256)
                keys = kv[both, :, at].reshape(GROUP, 256)
                values = kv[both, :, width + h * 256:width + h * 256 + 256].reshape(GROUP, 256)
                qh = q[row, at]
                q2 = jnp.concatenate([jnp.concatenate([qh[:, :128], zero], 1), jnp.concatenate([zero, qh[:, 128:]], 1)], 0)
                scores = lax.dot_general(keys, q2, (((1,), (1,)), ((), ())), preferred_element_type=jnp.float32)
                top = jnp.max(scores, axis=0, keepdims=True)
                expd = jnp.exp2((scores - top) * SCALE)
                probs = (expd * (1.0 / jnp.sum(expd, axis=0, keepdims=True))).astype(jnp.bfloat16)
                mixed = lax.dot_general(probs, values, (((0,), (0,)), ((), ())), preferred_element_type=jnp.float32)
                o[row, at] = jnp.concatenate([mixed[:GROUP, :128], mixed[GROUP:, 128:]], 1).astype(jnp.bfloat16)
        o_copy(i).start()
        return 0

    lax.fori_loop(0, chunks, step, 0)
    for i in range(chunks):
        o_copy(i).wait()


def attend(slots, queries, kv, chunk=8):
    chunks = queries.shape[0] // GROUP // chunk
    hbm = pl.BlockSpec(memory_space=pltpu.HBM)
    dma = pltpu.SemaphoreType.DMA
    return pl.pallas_call(
        functools.partial(attend_kernel, chunk),
        out_shape=jax.ShapeDtypeStruct(queries.shape, queries.dtype),
        in_specs=[pl.BlockSpec(memory_space=pltpu.SMEM), hbm, hbm],
        out_specs=hbm,
        scratch_shapes=[pltpu.VMEM(queries.shape, jnp.bfloat16), pltpu.VMEM(kv.shape, jnp.bfloat16),
                        pltpu.VMEM(queries.shape, jnp.bfloat16), dma((chunks,)), dma((chunks,)), dma((chunks,))],
        compiler_params=pltpu.CompilerParams(vmem_limit_bytes=58 << 20),
        cost_estimate=pl.CostEstimate(flops=4 * queries.size * GROUP, bytes_accessed=17 << 20, transcendentals=queries.size // 2),
    )(slots, queries, kv)


def body(ny, queries, encoded, w_kv, retrieved):
    nz = lax.axis_size("seq") // (ny * CORES)
    seq = lax.axis_index("seq")
    z, y, c = seq // (ny * CORES), (seq // CORES) % ny, seq % CORES
    inner, _, width = w_kv.shape
    weights = w_kv.reshape(inner, 2, width // 128, 128).transpose(0, 2, 1, 3).reshape(-1, 128)
    owner = retrieved.reshape(-1) // TILES
    k = (z - owner // (ny * CORES)) % nz
    step = jnp.where(k == 0, 0, jnp.where(k <= nz // 2, 2 * k - 1, 2 * (nz - k)))
    slots = (step * CORES + (c - owner) % CORES) * ny + (y - owner // CORES) % ny
    kv = gather_and_project(retrieved.T, encoded, weights, nz, ny)
    return attend(slots.astype(jnp.int32), queries, kv)


def solution(mesh):
    in_specs = (P("seq", "mp"), P("seq", None, None), P(None, None, "mp"), P("seq", None))
    return jax.shard_map(functools.partial(body, 4), mesh=mesh, in_specs=in_specs, out_specs=P("seq", "mp"), check_vma=False)
```

time: 179 us -> 71.4 us (0.40)
  waiting for transfers between devices: 75.4 us -> 0 us
  Pallas kernels: 0 us -> 69.9 us
  local copies, waits for them, and re-layouts: 43.3 us -> 0.86 us
  blocking collectives: 22.3 us -> 0 us
  matrix products: 18.2 us -> 0 us
  other arithmetic: 13.1 us -> 0.52 us
  starting transfers between devices: 5.66 us -> 0 us
    all_to_all x1 -> x0, waiting for transfers between devices: 75.4 us -> none  [body(): lax.all_to_all(outgoing, 'seq', split_axis=0, concat_axis=0, tiled=True)]
    pallas_call x0 -> x2, Pallas kernels: none -> 69.9 us  [the longest x1 57.1 us: gather_and_project(): pl.pallas_call(functools.partial(gather_kernel, nz, ny), out_shape=jax.Sh...]
    unnamed x15 -> x1, local copies, waits for them, and re-layouts: 23.2 us -> 0.76 us
    all_to_all x1 -> x0, blocking collectives: 22.3 us -> none  [body(): lax.all_to_all(request, 'seq', split_axis=0, concat_axis=0, tiled=True)]
    dot_general x3 -> x0, matrix products: 18.2 us -> none  [the longest x1 10.9 us: project_rows(): jnp.dot(tiles.reshape(count * rows, width), weights, preferred_element_ty...]
    convert_element_type x1 -> x0, local copies, waits for them, and re-layouts: 8.14 us -> none  [body(): return mixed.astype(jnp.bfloat16).reshape(group_count * GROUP, local_width)]
    gather x2 -> x0, local copies, waits for them, and re-layouts: 7.68 us -> none  [the longest x1 4.89 us: body(): jnp.take(lax.all_to_all(outgoing, 'seq', split_axis=0, concat_axis=0, til...]
    select_n x5 -> x0, other arithmetic: 7.03 us -> none  [the longest x2 4.39 us: body(): outgoing = jnp.take(encoded, asked, axis=0)]
  transfers between devices with their start and end apart: 1 -> 0, of which waited for: 1 -> 0; matrix products, arithmetic and copies ran while one was open for 5% -> 0% of each run, Pallas kernels for 0% -> 0%
where the time goes in v1:
time: 71.4 us; the launch traced here: 71.3 us
  Pallas kernels  69.9 us (98%)
  local copies, waits for them, and re-layouts  0.86 us (1%)
    pallas_call x1, Pallas kernels, gather_and_project(): pl.pallas_call(functools.partial(gather_kernel, nz, ny), out_shape=jax.Sh...  57.1 us
    pallas_call x1, Pallas kernels, attend(): pl.pallas_call(functools.partial(attend_kernel, chunk), out_shape=jax.Sha...  12.8 us

profile of v1, /device:TPU:1, one launch (start us, length us, event | category | flops | bytes accessed | tf_op | source)
XLA Modules:
  0.0 71.3 jit_solution(5855492442595389789)
XLA Ops:
  0.0 0.8 %copy.7 = s32[32,2]{1,0:T(8,128)S(1)} copy(s32[32,2]{0,1:T(2,128)} %param.7) | data formatting | bytes 512 | tf_op args[3]
  0.8 0.1 reshape.12
  0.9 0.5 fusion.1.slots_ref
  1.4 57.1 %shard_map.46.kv_hbm = bf16[64,32,2048]{2,1,0:T(8,128)(2,1)} custom-call(s32[2,32]{1,0:T(2,128)} %bitcast.7, bf16[4,2,16,896]{3,2,1,0:T(8,128)(2,1)} %bitcast.9, bf16[14336,128]{1,0:T(8,128)(2,1)} %bitcast.8), custom_call_target="tpu_custom_call" | custom-call | flops 7516192768 | bytes 16777216 | tf_op jit(solution)/shard_map/pallas_call | solution.py:201
  58.5 12.8 %shard_map.47 = bf16[2048,1024]{1,0:T(8,128)(2,1)} custom-call(s32[64]{0:T(128)} %fusion.1.slots_ref, bf16[2048,1024]{1,0:T(8,128)(2,1)} %q_hbm.1, bf16[64,32,2048]{2,1,0:T(8,128)(2,1)} %shard_map.46.kv_hbm), custom_call_target="tpu_custom_call" | custom-call | flops 536870912 | bytes 17825792 | tf_op jit(solution)/shard_map/pallas_call | solution.py:276

commit v2 on v1

--- a/solution.py
+++ b/solution.py
@@ -12,6 +12,7 @@
 TILES = 4
 CORES = 2
 MESH = pl.DeviceIdType.MESH
+X_LAG, P_LAG = 2, 4
 SCALE = (HEAD_DIM ** -0.5) * 1.4426950408889634
 
 
@@ -78,6 +79,25 @@
         ids_copy(r).start()
     for step in range(1, nz):
         z_copy(step).start()
+
+    w_copy.wait()
+    kinds = w_flat.shape[1] // 128
+    per = 256 // kinds
+    out_row = lax.broadcasted_iota(jnp.int32, (256, 256), 0)
+    in_col = lax.broadcasted_iota(jnp.int32, (256, 256), 1)
+    order = jnp.where(in_col == out_row % per * kinds + out_row // per, 1.0, 0.0).astype(jnp.bfloat16)
+
+    def unweave(i, _):
+        for u in range(8):
+            b = i * 8 + u
+            block = w_raw[pl.ds(pl.multiple_of(b * 256, 256), 256), :]
+            sorted_rows = jnp.dot(order, block, preferred_element_type=jnp.float32).astype(jnp.bfloat16)
+            for kind in range(kinds):
+                at = (kind % 2) * (kinds // 2) + kind // 2
+                w_flat[pl.ds(pl.multiple_of(b * per, per), per), at * 128:at * 128 + 128] = sorted_rows[kind * per:(kind + 1) * per]
+        return 0
+
+    lax.fori_loop(0, w_raw.shape[0] // 2048, unweave, 0)
 
     steps = lax.broadcasted_iota(jnp.int32, (nz, 1), 0)
     owner = ((z + nz - step_distance(steps, nz)) % nz * ny + y) * CORES + c
@@ -108,25 +128,6 @@
     own_copy.wait()
     pick(0)
 
-    w_copy.wait()
-    kinds = w_flat.shape[1] // 128
-    per = 256 // kinds
-    out_row = lax.broadcasted_iota(jnp.int32, (256, 256), 0)
-    in_col = lax.broadcasted_iota(jnp.int32, (256, 256), 1)
-    order = jnp.where(in_col == out_row % per * kinds + out_row // per, 1.0, 0.0).astype(jnp.bfloat16)
-
-    def unweave(i, _):
-        for u in range(2):
-            b = i * 2 + u
-            block = w_raw[pl.ds(pl.multiple_of(b * 256, 256), 256), :]
-            sorted_rows = jnp.dot(order, block, preferred_element_type=jnp.float32).astype(jnp.bfloat16)
-            for kind in range(kinds):
-                at = (kind % 2) * (kinds // 2) + kind // 2
-                w_flat[pl.ds(pl.multiple_of(b * per, per), per), at * 128:at * 128 + 128] = sorted_rows[kind * per:(kind + 1) * per]
-        return 0
-
-    lax.fori_loop(0, w_raw.shape[0] // 512, unweave, 0)
-
     def kv_copy(step):
         return pltpu.make_async_copy(staged.at[step % 2], kv_ref.at[pl.ds(step * nr, nr)], kv_sem.at[step % 2])
 
@@ -155,21 +156,21 @@
             z_copy(i).wait_recv()
             pick(i)
 
-        @pl.when(i <= nz)
+        @pl.when((i >= X_LAG) & (i < nz + X_LAG))
         def _():
             for d in range(2):
                 for r in range(d * ny, (d + 1) * ny):
                     if r > 0:
-                        y_copy(i - 1, r).wait_recv()
-                x_copy(i - 1, d).start()
-
-        @pl.when(i >= 2)
-        def _():
-            project(i - 2)
+                        y_copy(i - X_LAG, r).wait_recv()
+                x_copy(i - X_LAG, d).start()
+
+        @pl.when(i >= P_LAG)
+        def _():
+            project(i - P_LAG)
 
         return 0
 
-    lax.fori_loop(1, nz + 2, body, 0)
+    lax.fori_loop(1, nz + P_LAG, body, 0)
 
     for step in range(nz - 2, nz):
         kv_copy(step).wait()
@@ -220,7 +221,7 @@
     )(ids, encoded.reshape(count, 2, rows // 2, width), weights)
 
 
-def attend_kernel(chunk, slots_ref, q_hbm, kv_hbm, o_hbm, q, kv, o, q_sem, kv_sem, o_sem):
+def attend_kernel(chunk, nz, ny, ids_ref, q_hbm, kv_hbm, o_hbm, q, kv, o, q_sem, kv_sem, o_sem):
     groups = q.shape[0] // GROUP
     chunks = groups // chunk
     width = q.shape[1]
@@ -234,10 +235,19 @@
         at = pl.ds(i * span, span)
         return pltpu.make_async_copy(o.at[at], o_hbm.at[at], o_sem.at[i])
 
+    seq = lax.axis_index("seq")
+    z, y, c = seq // (ny * CORES), (seq // CORES) % ny, seq % CORES
+
+    def slot_of(tile):
+        owner = tile // TILES
+        k = (z + nz - owner // (ny * CORES)) % nz
+        step = jnp.where(k == 0, 0, jnp.where(k <= nz // 2, 2 * k - 1, 2 * (nz - k)))
+        return (step * CORES + (c + owner) % CORES) * ny + (y + ny - owner // CORES % ny) % ny
+
     for i in range(chunks):
         q_copy(i).start()
         for j in range(2 * chunk * i, 2 * chunk * (i + 1)):
-            pltpu.make_async_copy(kv_hbm.at[slots_ref[j]], kv.at[j], kv_sem.at[i]).start()
+            pltpu.make_async_copy(kv_hbm.at[slot_of(ids_ref[j % 2, j // 2])], kv.at[j], kv_sem.at[i]).start()
 
     zero = jnp.zeros((GROUP, HEAD_DIM), jnp.bfloat16)
 
@@ -245,22 +255,25 @@
         q_copy(i).wait()
         part = kv.at[pl.ds(i * 2 * chunk, 2 * chunk)]
         pltpu.make_async_copy(part, part, kv_sem.at[i]).wait()
-        for u in range(chunk):
-            g = i * chunk + u
-            row = pl.ds(pl.multiple_of(g * GROUP, GROUP), GROUP)
-            both = pl.ds(2 * g, 2)
-            for h in range(width // 256):
-                at = slice(h * 256, h * 256 + 256)
-                keys = kv[both, :, at].reshape(GROUP, 256)
-                values = kv[both, :, width + h * 256:width + h * 256 + 256].reshape(GROUP, 256)
-                qh = q[row, at]
-                q2 = jnp.concatenate([jnp.concatenate([qh[:, :128], zero], 1), jnp.concatenate([zero, qh[:, 128:]], 1)], 0)
-                scores = lax.dot_general(keys, q2, (((1,), (1,)), ((), ())), preferred_element_type=jnp.float32)
-                top = jnp.max(scores, axis=0, keepdims=True)
-                expd = jnp.exp2((scores - top) * SCALE)
-                probs = (expd * (1.0 / jnp.sum(expd, axis=0, keepdims=True))).astype(jnp.bfloat16)
-                mixed = lax.dot_general(probs, values, (((0,), (0,)), ((), ())), preferred_element_type=jnp.float32)
-                o[row, at] = jnp.concatenate([mixed[:GROUP, :128], mixed[GROUP:, 128:]], 1).astype(jnp.bfloat16)
+        rows = [pl.ds(pl.multiple_of((i * chunk + u) * GROUP, GROUP), GROUP) for u in range(chunk)]
+        units = [(u, h * 256) for u in range(chunk) for h in range(width // 256)]
+
+        def tile_rows(u, at):
+            return kv[pl.ds(2 * (i * chunk + u), 2), :, at:at + 256].reshape(GROUP, 256)
+
+        all_scores = []
+        for u, at in units:
+            qh = q[rows[u], at:at + 256]
+            q2 = jnp.concatenate([jnp.concatenate([qh[:, :128], zero], 1), jnp.concatenate([zero, qh[:, 128:]], 1)], 0)
+            all_scores.append(lax.dot_general(tile_rows(u, at), q2, (((1,), (1,)), ((), ())), preferred_element_type=jnp.float32))
+        all_probs = []
+        for scores in all_scores:
+            top = jnp.max(scores, axis=0, keepdims=True)
+            expd = jnp.exp2((scores - top) * SCALE)
+            all_probs.append((expd * (1.0 / jnp.sum(expd, axis=0, keepdims=True))).astype(jnp.bfloat16))
+        for (u, at), probs in zip(units, all_probs):
+            mixed = lax.dot_general(probs, tile_rows(u, width + at), (((0,), (0,)), ((), ())), preferred_element_type=jnp.float32)
+            o[rows[u], at:at + 256] = jnp.concatenate([mixed[:GROUP, :128], mixed[GROUP:, 128:]], 1).astype(jnp.bfloat16)
         o_copy(i).start()
         return 0
 
@@ -269,12 +282,12 @@
         o_copy(i).wait()
 
 
-def attend(slots, queries, kv, chunk=8):
+def attend(ids, queries, kv, nz, ny, chunk=4):
     chunks = queries.shape[0] // GROUP // chunk
     hbm = pl.BlockSpec(memory_space=pltpu.HBM)
     dma = pltpu.SemaphoreType.DMA
     return pl.pallas_call(
-        functools.partial(attend_kernel, chunk),
+        functools.partial(attend_kernel, chunk, nz, ny),
         out_shape=jax.ShapeDtypeStruct(queries.shape, queries.dtype),
         in_specs=[pl.BlockSpec(memory_space=pltpu.SMEM), hbm, hbm],
         out_specs=hbm,
@@ -282,21 +295,16 @@
                         pltpu.VMEM(queries.shape, jnp.bfloat16), dma((chunks,)), dma((chunks,)), dma((chunks,))],
         compiler_params=pltpu.CompilerParams(vmem_limit_bytes=58 << 20),
         cost_estimate=pl.CostEstimate(flops=4 * queries.size * GROUP, bytes_accessed=17 << 20, transcendentals=queries.size // 2),
-    )(slots, queries, kv)
+    )(ids, queries, kv)
 
 
 def body(ny, queries, encoded, w_kv, retrieved):
     nz = lax.axis_size("seq") // (ny * CORES)
-    seq = lax.axis_index("seq")
-    z, y, c = seq // (ny * CORES), (seq // CORES) % ny, seq % CORES
     inner, _, width = w_kv.shape
     weights = w_kv.reshape(inner, 2, width // 128, 128).transpose(0, 2, 1, 3).reshape(-1, 128)
-    owner = retrieved.reshape(-1) // TILES
-    k = (z - owner // (ny * CORES)) % nz
-    step = jnp.where(k == 0, 0, jnp.where(k <= nz // 2, 2 * k - 1, 2 * (nz - k)))
-    slots = (step * CORES + (c - owner) % CORES) * ny + (y - owner // CORES) % ny
-    kv = gather_and_project(retrieved.T, encoded, weights, nz, ny)
-    return attend(slots.astype(jnp.int32), queries, kv)
+    ids = retrieved.T
+    kv = gather_and_project(ids, encoded, weights, nz, ny)
+    return attend(ids, queries, kv, nz, ny)
 
 
 def solution(mesh):

time: 71.4 us -> 60.6 us (0.85)
  Pallas kernels: 69.9 us -> 60.5 us
  local copies, waits for them, and re-layouts: 0.86 us -> 0 us
    pallas_call x1, Pallas kernels: 57.1 us -> 49 us  [gather_and_project(): pl.pallas_call(functools.partial(gather_kernel, nz, ny), out_shape=jax.Sh...]
    pallas_call x1, Pallas kernels: 12.8 us -> 11.5 us  [attend(): pl.pallas_call(functools.partial(attend_kernel, chunk, nz, ny), out_shape...]
    unnamed x1 -> x0, local copies, waits for them, and re-layouts: 0.76 us -> none
where the time goes in v2:
time: 60.6 us; the launch traced here: 60.5 us
  Pallas kernels  60.5 us (100%)
    pallas_call x1, Pallas kernels, gather_and_project(): pl.pallas_call(functools.partial(gather_kernel, nz, ny), out_shape=jax.Sh...  49 us
    pallas_call x1, Pallas kernels, attend(): pl.pallas_call(functools.partial(attend_kernel, chunk, nz, ny), out_shape...  11.5 us

profile of v2, /device:TPU:1, one launch (start us, length us, event | category | flops | bytes accessed | tf_op | source)
XLA Modules:
  0.0 60.5 jit_solution(3631956946162942230)
XLA Ops:
  0.0 49.0 %shard_map.46.kv_hbm = bf16[64,32,2048]{2,1,0:T(8,128)(2,1)} custom-call(s32[2,32]{1,0:T(2,128)} %bitcast.7, bf16[4,2,16,896]{3,2,1,0:T(8,128)(2,1)} %bitcast.10, bf16[14336,128]{1,0:T(8,128)(2,1)} %bitcast.9), custom_call_target="tpu_custom_call" | custom-call | flops 7516192768 | bytes 16777216 | tf_op jit(solution)/shard_map/pallas_call | solution.py:202
  49.0 11.5 %shard_map.47 = bf16[2048,1024]{1,0:T(8,128)(2,1)} custom-call(s32[2,32]{1,0:T(2,128)} %bitcast.8, bf16[2048,1024]{1,0:T(8,128)(2,1)} %q_hbm.1, bf16[64,32,2048]{2,1,0:T(8,128)(2,1)} %shard_map.46.kv_hbm), custom_call_target="tpu_custom_call" | custom-call | flops 536870912 | bytes 17825792 | tf_op jit(solution)/shard_map/pallas_call | solution.py:289

commit v3 on v2

--- a/solution.py
+++ b/solution.py
@@ -21,8 +21,8 @@
 
 
 def gather_kernel(nz, ny, ids_ref, enc_ref, w_ref, kv_ref,
-                  ids_in, sel, pool, picked, rows, w_raw, w_flat, staged,
-                  ids_send, ids_recv, z_send, z_recv, y_send, y_recv, x_send, x_recv, own_sem, w_sem, kv_sem):
+                  ids_in, sel, pool, picked, rows, w_raw, w_flat,
+                  ids_send, ids_recv, z_send, z_recv, y_send, y_recv, x_send, x_recv, own_sem, w_sem):
     seq, x = lax.axis_index("seq"), lax.axis_index("mp")
     nx = lax.axis_size("mp")
     z, y, c = seq // (ny * CORES), (seq // CORES) % ny, seq % CORES
@@ -128,27 +128,19 @@
     own_copy.wait()
     pick(0)
 
-    def kv_copy(step):
-        return pltpu.make_async_copy(staged.at[step % 2], kv_ref.at[pl.ds(step * nr, nr)], kv_sem.at[step % 2])
-
     def project(step):
         for d in range(2):
             x_arrival(step, d).wait_recv()
 
-        @pl.when(step >= 2)
-        def _():
-            kv_copy(step - 2).wait()
-
         flat = rows[step].reshape(nr * 32, rows.shape[-1])
 
         def columns(i, _):
             at = pl.ds(pl.multiple_of(i * 512, 512), 512)
             part = jnp.dot(flat, w_flat[:, at], preferred_element_type=jnp.float32).astype(jnp.bfloat16)
-            staged[step % 2, :, :, at] = part.reshape(nr, 32, 512)
+            kv_ref[pl.ds(step * nr, nr), :, at] = part.reshape(nr, 32, 512)
             return 0
 
         lax.fori_loop(0, w_flat.shape[1] // 512, columns, 0)
-        kv_copy(step).start()
 
     def body(i, _):
         @pl.when(i < nz)
@@ -172,8 +164,6 @@
 
     lax.fori_loop(1, nz + P_LAG, body, 0)
 
-    for step in range(nz - 2, nz):
-        kv_copy(step).wait()
     for r in range(1, nr):
         ids_copy(r).wait_send()
 
@@ -192,7 +182,7 @@
 
 
 def gather_and_project(ids, encoded, weights, nz, ny):
-    count, rows, width = encoded.shape
+    rows, width = 2 * encoded.shape[2], encoded.shape[3]
     nr = ny * CORES
     features = weights.shape[0] * 128 // width
     dma = pltpu.SemaphoreType.DMA
@@ -203,7 +193,7 @@
         functools.partial(gather_kernel, nz, ny),
         out_shape=jax.ShapeDtypeStruct((slots, rows, features), bf16),
         in_specs=[pl.BlockSpec(memory_space=pltpu.VMEM), hbm, hbm],
-        out_specs=hbm,
+        out_specs=pl.BlockSpec(memory_space=pltpu.VMEM),
         scratch_shapes=[
             pltpu.VMEM((nr,) + ids.shape, jnp.int32),
             pltpu.VMEM((nr, TILES, nz, 128), jnp.float32),
@@ -212,24 +202,19 @@
             pltpu.VMEM((nz, nr, 2, 16, width), bf16),
             pltpu.VMEM(weights.shape, bf16),
             pltpu.VMEM((width, features), bf16),
-            pltpu.VMEM((2, nr, rows, features), bf16),
             dma((nr,)), dma((nr,)), dma((nz,)), dma((nz,)), dma((nz, nr)), dma((nz, nr)), dma((nz, 2)), dma((nz, 2)),
-            dma, dma, dma((2,)),
+            dma, dma,
         ],
-        compiler_params=pltpu.CompilerParams(collective_id=0, has_side_effects=True, vmem_limit_bytes=58 << 20),
+        compiler_params=pltpu.CompilerParams(collective_id=0, has_side_effects=True, vmem_limit_bytes=20 << 20),
         cost_estimate=pl.CostEstimate(flops=2 * slots * rows * width * features, bytes_accessed=16 << 20, transcendentals=0),
-    )(ids, encoded.reshape(count, 2, rows // 2, width), weights)
-
-
-def attend_kernel(chunk, nz, ny, ids_ref, q_hbm, kv_hbm, o_hbm, q, kv, o, q_sem, kv_sem, o_sem):
+    )(ids, encoded, weights)
+
+
+def attend_kernel(chunk, nz, ny, ids_ref, q, kv, o_hbm, o, o_sem):
     groups = q.shape[0] // GROUP
     chunks = groups // chunk
     width = q.shape[1]
     span = chunk * GROUP
-
-    def q_copy(i):
-        at = pl.ds(i * span, span)
-        return pltpu.make_async_copy(q_hbm.at[at], q.at[at], q_sem.at[i])
 
     def o_copy(i):
         at = pl.ds(i * span, span)
@@ -244,22 +229,15 @@
         step = jnp.where(k == 0, 0, jnp.where(k <= nz // 2, 2 * k - 1, 2 * (nz - k)))
         return (step * CORES + (c + owner) % CORES) * ny + (y + ny - owner // CORES % ny) % ny
 
-    for i in range(chunks):
-        q_copy(i).start()
-        for j in range(2 * chunk * i, 2 * chunk * (i + 1)):
-            pltpu.make_async_copy(kv_hbm.at[slot_of(ids_ref[j % 2, j // 2])], kv.at[j], kv_sem.at[i]).start()
-
     zero = jnp.zeros((GROUP, HEAD_DIM), jnp.bfloat16)
 
     def step(i, _):
-        q_copy(i).wait()
-        part = kv.at[pl.ds(i * 2 * chunk, 2 * chunk)]
-        pltpu.make_async_copy(part, part, kv_sem.at[i]).wait()
+        slots = [[slot_of(ids_ref[j, i * chunk + u]) for j in range(2)] for u in range(chunk)]
         rows = [pl.ds(pl.multiple_of((i * chunk + u) * GROUP, GROUP), GROUP) for u in range(chunk)]
         units = [(u, h * 256) for u in range(chunk) for h in range(width // 256)]
 
         def tile_rows(u, at):
-            return kv[pl.ds(2 * (i * chunk + u), 2), :, at:at + 256].reshape(GROUP, 256)
+            return jnp.concatenate([kv[slot, :, at:at + 256] for slot in slots[u]], 0)
 
         all_scores = []
         for u, at in units:
@@ -282,18 +260,18 @@
         o_copy(i).wait()
 
 
-def attend(ids, queries, kv, nz, ny, chunk=4):
+def attend(ids, queries, kv, nz, ny, chunk=8):
     chunks = queries.shape[0] // GROUP // chunk
+    vmem = pl.BlockSpec(memory_space=pltpu.VMEM)
     hbm = pl.BlockSpec(memory_space=pltpu.HBM)
     dma = pltpu.SemaphoreType.DMA
     return pl.pallas_call(
         functools.partial(attend_kernel, chunk, nz, ny),
         out_shape=jax.ShapeDtypeStruct(queries.shape, queries.dtype),
-        in_specs=[pl.BlockSpec(memory_space=pltpu.SMEM), hbm, hbm],
+        in_specs=[pl.BlockSpec(memory_space=pltpu.SMEM), vmem, vmem],
         out_specs=hbm,
-        scratch_shapes=[pltpu.VMEM(queries.shape, jnp.bfloat16), pltpu.VMEM(kv.shape, jnp.bfloat16),
-                        pltpu.VMEM(queries.shape, jnp.bfloat16), dma((chunks,)), dma((chunks,)), dma((chunks,))],
-        compiler_params=pltpu.CompilerParams(vmem_limit_bytes=58 << 20),
+        scratch_shapes=[pltpu.VMEM(queries.shape, jnp.bfloat16), dma((chunks,))],
+        compiler_params=pltpu.CompilerParams(vmem_limit_bytes=20 << 20),
         cost_estimate=pl.CostEstimate(flops=4 * queries.size * GROUP, bytes_accessed=17 << 20, transcendentals=queries.size // 2),
     )(ids, queries, kv)
 
@@ -303,7 +281,8 @@
     inner, _, width = w_kv.shape
     weights = w_kv.reshape(inner, 2, width // 128, 128).transpose(0, 2, 1, 3).reshape(-1, 128)
     ids = retrieved.T
-    kv = gather_and_project(ids, encoded, weights, nz, ny)
+    kv = gather_and_project(ids, pltpu.with_memory_space_constraint(encoded.reshape(encoded.shape[0], 2, -1, inner), pltpu.HBM),
+                            pltpu.with_memory_space_constraint(weights, pltpu.HBM), nz, ny)
     return attend(ids, queries, kv, nz, ny)
 
 

time: 60.6 us -> 55.5 us (0.916)
  Pallas kernels: 60.5 us -> 54.7 us
  local copies, waits for them, and re-layouts: 0 us -> 0.68 us
    pallas_call x1, Pallas kernels: 11.5 us -> 7.27 us  [attend(): pl.pallas_call(functools.partial(attend_kernel, chunk, nz, ny), out_shape...]
    pallas_call x1, Pallas kernels: 49 us -> 47.4 us  [gather_and_project(): pl.pallas_call(functools.partial(gather_kernel, nz, ny), out_shape=jax.Sh...]
    unnamed x0 -> x4, local copies, waits for them, and re-layouts: none -> 0.68 us
where the time goes in v3:
time: 55.5 us; the launch traced here: 55.4 us
  Pallas kernels  54.7 us (99%)
  local copies, waits for them, and re-layouts  0.68 us (1%)
    pallas_call x1, Pallas kernels, gather_and_project(): pl.pallas_call(functools.partial(gather_kernel, nz, ny), out_shape=jax.Sh...  47.4 us
    pallas_call x1, Pallas kernels, attend(): pl.pallas_call(functools.partial(attend_kernel, chunk, nz, ny), out_shape...  7.27 us

profile of v3, /device:TPU:1, one launch (start us, length us, event | category | flops | bytes accessed | tf_op | source)
XLA Modules:
  0.0 55.4 jit_solution(14869259637704043625)
XLA Ops:
  0.0 0.0 copy-start.1
  0.0 0.7 %copy-done.1 = s32[32,2]{0,1:T(2,128)S(1)} copy-done((s32[32,2]{0,1:T(2,128)S(1)}, s32[32,2]{0,1:T(2,128)}, u32[]{:S(2)}) %copy-start.1) | copy-done | bytes 280
  0.7 0.0 copy-start
  0.7 47.4 %shard_map.46.kv = bf16[64,32,2048]{2,1,0:T(8,128)(2,1)S(1)} custom-call(s32[2,32]{1,0:T(2,128)S(1)} %bitcast.7, bf16[4,2,16,896]{3,2,1,0:T(8,128)(2,1)} %bitcast.10, bf16[14336,128]{1,0:T(8,128)(2,1)} %bitcast.9), custom_call_target="tpu_custom_call" | custom-call | flops 7516192768 | bytes 16777216 | tf_op jit(solution)/shard_map/pallas_call | solution.py:192
  48.1 0.0 copy-done
  48.1 7.3 %shard_map.47 = bf16[2048,1024]{1,0:T(8,128)(2,1)} custom-call(s32[2,32]{1,0:T(2,128)S(1)} %bitcast.8, bf16[2048,1024]{1,0:T(8,128)(2,1)S(1)} %copy-done, bf16[64,32,2048]{2,1,0:T(8,128)(2,1)S(1)} %shard_map.46.kv), custom_call_target="tpu_custom_call" | custom-call | flops 536870912 | bytes 17825792 | tf_op jit(solution)/shard_map/pallas_call | solution.py:268
Async XLA Ops:
  0.0 0.7 %copy-start.1 = (s32[32,2]{0,1:T(2,128)S(1)}, s32[32,2]{0,1:T(2,128)}, u32[]{:S(2)}) copy-start(s32[32,2]{0,1:T(2,128)} %param.7) | copy-start | bytes 772
  0.7 47.4 %copy-start = (bf16[2048,1024]{1,0:T(8,128)(2,1)S(1)}, bf16[2048,1024]{1,0:T(8,128)(2,1)}, u32[]{:S(2)}) copy-start(bf16[2048,1024]{1,0:T(8,128)(2,1)} %q.1) | copy-start | bytes 12582916

commit v4 on v3

--- a/solution.py
+++ b/solution.py
@@ -17,12 +17,18 @@
 
 
 def step_distance(step, nz):
-    return jnp.where(step % 2 == 1, (step + 1) // 2, (nz - step // 2) % nz)
-
-
-def gather_kernel(nz, ny, ids_ref, enc_ref, w_ref, kv_ref,
-                  ids_in, sel, pool, picked, rows, w_raw, w_flat,
-                  ids_send, ids_recv, z_send, z_recv, y_send, y_recv, x_send, x_recv, own_sem, w_sem):
+    near = jnp.where(step % 2 == 1, (step + 1) // 2, (nz - step // 2) % nz)
+    return jnp.where(step < 5, near, jnp.where(step == 5, nz // 2, jnp.where(step == 6, 3, nz - 3)))
+
+
+def distance_step(k, nz):
+    near = jnp.where(k == 0, 0, jnp.where(k <= 2, 2 * k - 1, 2 * (nz - k)))
+    return jnp.where(k == nz // 2, 5, jnp.where(k == 3, 6, jnp.where(k == nz - 3, 7, near)))
+
+
+def gather_kernel(nz, ny, ids_hbm, enc_ref, w_ref, kv_ref,
+                  ids_ref, ids_in, sel, pool, picked, rows, w_raw, w_flat,
+                  ids_send, ids_recv, z_send, z_recv, y_send, y_recv, x_send, x_recv, own_sem, w_sem, ids_sem):
     seq, x = lax.axis_index("seq"), lax.axis_index("mp")
     nx = lax.axis_size("mp")
     z, y, c = seq // (ny * CORES), (seq // CORES) % ny, seq % CORES
@@ -39,8 +45,10 @@
     def in_row_back(r):
         return ((z * ny + (y + ny - r % ny) % ny) * CORES + (c + r // ny) % CORES, x)
 
+    ids_load = pltpu.make_async_copy(ids_hbm, ids_ref, ids_sem)
+    ids_load.start()
     barrier = pltpu.get_barrier_semaphore()
-    for k in range(1, nz):
+    for k in (1, nz - 1, 2, nz - 2, nz // 2):
         pl.semaphore_signal(barrier, inc=1, device_id=along_z(k), device_id_type=MESH)
     for r in range(1, nr):
         pl.semaphore_signal(barrier, inc=1, device_id=in_row(r), device_id_type=MESH)
@@ -50,7 +58,8 @@
     own_copy.start()
     w_copy = pltpu.make_async_copy(w_ref, w_raw, w_sem)
     w_copy.start()
-    pl.semaphore_wait(barrier, nz + nr)
+    ids_load.wait()
+    pl.semaphore_wait(barrier, 5 + (nr - 1) + 2)
 
     def ids_copy(r):
         return pltpu.make_async_remote_copy(ids_ref, ids_in.at[r], ids_send.at[r], ids_recv.at[r],
@@ -61,6 +70,10 @@
         return pltpu.make_async_remote_copy(enc_ref.at[:, half], pool.at[step], z_send.at[step], z_recv.at[step],
                                             device_id=along_z(k), device_id_type=MESH)
 
+    def pass_on(step):
+        return pltpu.make_async_remote_copy(pool.at[step], pool.at[step + 3], z_send.at[step + 3], z_recv.at[step + 3],
+                                            device_id=along_z(jnp.where(step == 3, 1, nz - 1)), device_id_type=MESH)
+
     def y_copy(step, r):
         return pltpu.make_async_remote_copy(picked.at[step, r], rows.at[step, r, half], y_send.at[step, r],
                                             y_recv.at[step, r], device_id=in_row(r), device_id_type=MESH)
@@ -77,7 +90,7 @@
 
     for r in range(1, nr):
         ids_copy(r).start()
-    for step in range(1, nz):
+    for step in range(1, 6):
         z_copy(step).start()
 
     w_copy.wait()
@@ -146,6 +159,11 @@
         @pl.when(i < nz)
         def _():
             z_copy(i).wait_recv()
+
+            @pl.when((i == 3) | (i == 4))
+            def _():
+                pass_on(i).start()
+
             pick(i)
 
         @pl.when((i >= X_LAG) & (i < nz + X_LAG))
@@ -192,9 +210,10 @@
     return pl.pallas_call(
         functools.partial(gather_kernel, nz, ny),
         out_shape=jax.ShapeDtypeStruct((slots, rows, features), bf16),
-        in_specs=[pl.BlockSpec(memory_space=pltpu.VMEM), hbm, hbm],
+        in_specs=[hbm, hbm, hbm],
         out_specs=pl.BlockSpec(memory_space=pltpu.VMEM),
         scratch_shapes=[
+            pltpu.VMEM(ids.shape, jnp.int32),
             pltpu.VMEM((nr,) + ids.shape, jnp.int32),
             pltpu.VMEM((nr, TILES, nz, 128), jnp.float32),
             pltpu.VMEM((nz, TILES, 16, width), bf16),
@@ -203,7 +222,7 @@
             pltpu.VMEM(weights.shape, bf16),
             pltpu.VMEM((width, features), bf16),
             dma((nr,)), dma((nr,)), dma((nz,)), dma((nz,)), dma((nz, nr)), dma((nz, nr)), dma((nz, 2)), dma((nz, 2)),
-            dma, dma,
+            dma, dma, dma,
         ],
         compiler_params=pltpu.CompilerParams(collective_id=0, has_side_effects=True, vmem_limit_bytes=20 << 20),
         cost_estimate=pl.CostEstimate(flops=2 * slots * rows * width * features, bytes_accessed=16 << 20, transcendentals=0),
@@ -226,8 +245,7 @@
     def slot_of(tile):
         owner = tile // TILES
         k = (z + nz - owner // (ny * CORES)) % nz
-        step = jnp.where(k == 0, 0, jnp.where(k <= nz // 2, 2 * k - 1, 2 * (nz - k)))
-        return (step * CORES + (c + owner) % CORES) * ny + (y + ny - owner // CORES % ny) % ny
+        return (distance_step(k, nz) * CORES + (c + owner) % CORES) * ny + (y + ny - owner // CORES % ny) % ny
 
     zero = jnp.zeros((GROUP, HEAD_DIM), jnp.bfloat16)
 
@@ -280,9 +298,9 @@
     nz = lax.axis_size("seq") // (ny * CORES)
     inner, _, width = w_kv.shape
     weights = w_kv.reshape(inner, 2, width // 128, 128).transpose(0, 2, 1, 3).reshape(-1, 128)
-    ids = retrieved.T
-    kv = gather_and_project(ids, pltpu.with_memory_space_constraint(encoded.reshape(encoded.shape[0], 2, -1, inner), pltpu.HBM),
-                            pltpu.with_memory_space_constraint(weights, pltpu.HBM), nz, ny)
+    in_hbm = functools.partial(pltpu.with_memory_space_constraint, memory_space=pltpu.HBM)
+    ids = in_hbm(retrieved.T)
+    kv = gather_and_project(ids, in_hbm(encoded.reshape(encoded.shape[0], 2, -1, inner)), in_hbm(weights), nz, ny)
     return attend(ids, queries, kv, nz, ny)
 
 

time: 55.5 us -> 52.7 us (0.950)
  Pallas kernels: 54.7 us -> 52.6 us
  local copies, waits for them, and re-layouts: 0.68 us -> 0.01 us
    pallas_call x1, Pallas kernels: 47.4 us -> 45.6 us  [gather_and_project(): pl.pallas_call(functools.partial(gather_kernel, nz, ny), out_shape=jax.Sh...]
    unnamed x4 -> x2, local copies, waits for them, and re-layouts: 0.68 us -> 0.01 us
where the time goes in v4:
time: 52.7 us; the launch traced here: 52.6 us
  Pallas kernels  52.6 us (100%)
    pallas_call x1, Pallas kernels, gather_and_project(): pl.pallas_call(functools.partial(gather_kernel, nz, ny), out_shape=jax.Sh...  45.6 us
    pallas_call x1, Pallas kernels, attend(): pl.pallas_call(functools.partial(attend_kernel, chunk, nz, ny), out_shape...  7.04 us

profile of v4, /device:TPU:1, one launch (start us, length us, event | category | flops | bytes accessed | tf_op | source)
XLA Modules:
  0.0 52.6 jit_solution(3860553952316424624)
XLA Ops:
  0.0 0.0 copy-start
  0.0 45.6 %shard_map.46.kv = bf16[64,32,2048]{2,1,0:T(8,128)(2,1)S(1)} custom-call(s32[2,32]{1,0:T(2,128)} %bitcast.7, bf16[4,2,16,896]{3,2,1,0:T(8,128)(2,1)} %bitcast.10, bf16[14336,128]{1,0:T(8,128)(2,1)} %bitcast.9), custom_call_target="tpu_custom_call" | custom-call | flops 7516192768 | bytes 16777216 | tf_op jit(solution)/shard_map/pallas_call | solution.py:210
  45.6 0.0 copy-done
  45.6 7.0 %shard_map.47 = bf16[2048,1024]{1,0:T(8,128)(2,1)} custom-call(s32[2,32]{1,0:T(2,128)} %bitcast.8, bf16[2048,1024]{1,0:T(8,128)(2,1)S(1)} %copy-done, bf16[64,32,2048]{2,1,0:T(8,128)(2,1)S(1)} %shard_map.46.kv), custom_call_target="tpu_custom_call" | custom-call | flops 536870912 | bytes 17825792 | tf_op jit(solution)/shard_map/pallas_call | solution.py:286
Async XLA Ops:
  0.0 45.6 %copy-start = (bf16[2048,1024]{1,0:T(8,128)(2,1)S(1)}, bf16[2048,1024]{1,0:T(8,128)(2,1)}, u32[]{:S(2)}) copy-start(bf16[2048,1024]{1,0:T(8,128)(2,1)} %q.1) | copy-start | bytes 12582916

commit v5 on v4

--- a/solution.py
+++ b/solution.py
@@ -27,7 +27,7 @@
 
 
 def gather_kernel(nz, ny, ids_hbm, enc_ref, w_ref, kv_ref,
-                  ids_ref, ids_in, sel, pool, picked, rows, w_raw, w_flat,
+                  ids_ref, ids_in, sel, pool, picked, mine, theirs, w_raw, w_flat,
                   ids_send, ids_recv, z_send, z_recv, y_send, y_recv, x_send, x_recv, own_sem, w_sem, ids_sem):
     seq, x = lax.axis_index("seq"), lax.axis_index("mp")
     nx = lax.axis_size("mp")
@@ -75,17 +75,12 @@
                                             device_id=along_z(jnp.where(step == 3, 1, nz - 1)), device_id_type=MESH)
 
     def y_copy(step, r):
-        return pltpu.make_async_remote_copy(picked.at[step, r], rows.at[step, r, half], y_send.at[step, r],
+        return pltpu.make_async_remote_copy(picked.at[step, r], mine.at[step, r], y_send.at[step, r],
                                             y_recv.at[step, r], device_id=in_row(r), device_id_type=MESH)
 
     def x_copy(step, d):
-        part = rows.at[step, pl.ds(d * ny, ny), half]
-        return pltpu.make_async_remote_copy(part, part, x_send.at[step, d], x_recv.at[step, d],
-                                            device_id=(right, left)[d], device_id_type=MESH)
-
-    def x_arrival(step, d):
-        part = rows.at[step, pl.ds(d * ny, ny), 1 - half]
-        return pltpu.make_async_remote_copy(part, part, x_send.at[step, d], x_recv.at[step, d],
+        at = pl.ds(d * ny, ny)
+        return pltpu.make_async_remote_copy(mine.at[step, at], theirs.at[step, at], x_send.at[step, d], x_recv.at[step, d],
                                             device_id=(right, left)[d], device_id_type=MESH)
 
     for r in range(1, nr):
@@ -133,7 +128,7 @@
                 term = tiles[t] * jnp.concatenate([lane] * width, axis=1)
                 total = term if total is None else total + term
             if r == 0:
-                rows[step, 0, half] = total
+                mine[step, 0] = total
             else:
                 picked[step, r] = total
                 y_copy(step, r).start()
@@ -141,19 +136,17 @@
     own_copy.wait()
     pick(0)
 
-    def project(step):
-        for d in range(2):
-            x_arrival(step, d).wait_recv()
-
-        flat = rows[step].reshape(nr * 32, rows.shape[-1])
+    def project(step, part, first):
+        flat = part[step].reshape(nr * 16, part.shape[-1])
+        span = w_flat.shape[1] // 2
 
         def columns(i, _):
-            at = pl.ds(pl.multiple_of(i * 512, 512), 512)
-            part = jnp.dot(flat, w_flat[:, at], preferred_element_type=jnp.float32).astype(jnp.bfloat16)
-            kv_ref[pl.ds(step * nr, nr), :, at] = part.reshape(nr, 32, 512)
+            at = pl.ds(pl.multiple_of(i * span, span), span)
+            out = jnp.dot(flat, w_flat[:, at], preferred_element_type=jnp.float32).astype(jnp.bfloat16)
+            kv_ref[pl.ds(step * nr, nr), first:first + 16, at] = out.reshape(nr, 16, span)
             return 0
 
-        lax.fori_loop(0, w_flat.shape[1] // 512, columns, 0)
+        lax.fori_loop(0, 2, columns, 0)
 
     def body(i, _):
         @pl.when(i < nz)
@@ -173,10 +166,13 @@
                     if r > 0:
                         y_copy(i - X_LAG, r).wait_recv()
                 x_copy(i - X_LAG, d).start()
+            project(i - X_LAG, mine, 0)
 
         @pl.when(i >= P_LAG)
         def _():
-            project(i - P_LAG)
+            for d in range(2):
+                x_copy(i - P_LAG, d).wait_recv()
+            project(i - P_LAG, theirs, 16)
 
         return 0
 
@@ -218,7 +214,8 @@
             pltpu.VMEM((nr, TILES, nz, 128), jnp.float32),
             pltpu.VMEM((nz, TILES, 16, width), bf16),
             pltpu.VMEM((nz, nr, 16, width), bf16),
-            pltpu.VMEM((nz, nr, 2, 16, width), bf16),
+            pltpu.VMEM((nz, nr, 16, width), bf16),
+            pltpu.VMEM((nz, nr, 16, width), bf16),
             pltpu.VMEM(weights.shape, bf16),
             pltpu.VMEM((width, features), bf16),
             dma((nr,)), dma((nr,)), dma((nz,)), dma((nz,)), dma((nz, nr)), dma((nz, nr)), dma((nz, 2)), dma((nz, 2)),

time: 52.7 us -> 51 us (0.968)
  Pallas kernels: 52.6 us -> 50.9 us
    pallas_call x1, Pallas kernels: 45.6 us -> 43.8 us  [gather_and_project(): pl.pallas_call(functools.partial(gather_kernel, nz, ny), out_shape=jax.Sh...]
where the time goes in v5:
time: 51 us; the launch traced here: 50.9 us
  Pallas kernels  50.9 us (100%)
    pallas_call x1, Pallas kernels, gather_and_project(): pl.pallas_call(functools.partial(gather_kernel, nz, ny), out_shape=jax.Sh...  43.8 us
    pallas_call x1, Pallas kernels, attend(): pl.pallas_call(functools.partial(attend_kernel, chunk, nz, ny), out_shape...  7.04 us

profile of v5, /device:TPU:1, one launch (start us, length us, event | category | flops | bytes accessed | tf_op | source)
XLA Modules:
  0.0 50.9 jit_solution(17066538204902195100)
XLA Ops:
  0.0 0.0 copy-start
  0.0 43.8 %shard_map.46.kv = bf16[64,32,2048]{2,1,0:T(8,128)(2,1)S(1)} custom-call(s32[2,32]{1,0:T(2,128)} %bitcast.7, bf16[4,2,16,896]{3,2,1,0:T(8,128)(2,1)} %bitcast.10, bf16[14336,128]{1,0:T(8,128)(2,1)} %bitcast.9), custom_call_target="tpu_custom_call" | custom-call | flops 7516192768 | bytes 16777216 | tf_op jit(solution)/shard_map/pallas_call | solution.py:206
  43.9 0.0 copy-done
  43.9 7.0 %shard_map.47 = bf16[2048,1024]{1,0:T(8,128)(2,1)} custom-call(s32[2,32]{1,0:T(2,128)} %bitcast.8, bf16[2048,1024]{1,0:T(8,128)(2,1)S(1)} %copy-done, bf16[64,32,2048]{2,1,0:T(8,128)(2,1)S(1)} %shard_map.46.kv), custom_call_target="tpu_custom_call" | custom-call | flops 536870912 | bytes 17825792 | tf_op jit(solution)/shard_map/pallas_call | solution.py:283
Async XLA Ops:
  0.0 43.9 %copy-start = (bf16[2048,1024]{1,0:T(8,128)(2,1)S(1)}, bf16[2048,1024]{1,0:T(8,128)(2,1)}, u32[]{:S(2)}) copy-start(bf16[2048,1024]{1,0:T(8,128)(2,1)} %q.1) | copy-start | bytes 12582916

commit v6 on v5

--- a/solution.py
+++ b/solution.py
@@ -79,9 +79,9 @@
                                             y_recv.at[step, r], device_id=in_row(r), device_id_type=MESH)
 
     def x_copy(step, d):
-        at = pl.ds(d * ny, ny)
+        at = pl.ds(d * ny + 1, ny - 1) if d < 2 else pl.ds((d - 2) * ny, 1)
         return pltpu.make_async_remote_copy(mine.at[step, at], theirs.at[step, at], x_send.at[step, d], x_recv.at[step, d],
-                                            device_id=(right, left)[d], device_id_type=MESH)
+                                            device_id=(right, left)[d % 2], device_id_type=MESH)
 
     for r in range(1, nr):
         ids_copy(r).start()
@@ -129,6 +129,7 @@
                 total = term if total is None else total + term
             if r == 0:
                 mine[step, 0] = total
+                x_copy(step, 2).start()
             else:
                 picked[step, r] = total
                 y_copy(step, r).start()
@@ -159,18 +160,23 @@
 
             pick(i)
 
+        @pl.when(i <= nz)
+        def _():
+            y_copy(i - 1, ny).wait_recv()
+            x_copy(i - 1, 3).start()
+
         @pl.when((i >= X_LAG) & (i < nz + X_LAG))
         def _():
             for d in range(2):
                 for r in range(d * ny, (d + 1) * ny):
-                    if r > 0:
+                    if r % ny > 0:
                         y_copy(i - X_LAG, r).wait_recv()
                 x_copy(i - X_LAG, d).start()
             project(i - X_LAG, mine, 0)
 
         @pl.when(i >= P_LAG)
         def _():
-            for d in range(2):
+            for d in range(4):
                 x_copy(i - P_LAG, d).wait_recv()
             project(i - P_LAG, theirs, 16)
 
@@ -188,7 +194,7 @@
 
         for r in range(1, nr):
             y_copy(step, r).wait_send()
-        for d in range(2):
+        for d in range(4):
             x_copy(step, d).wait_send()
         return 0
 
@@ -218,7 +224,7 @@
             pltpu.VMEM((nz, nr, 16, width), bf16),
             pltpu.VMEM(weights.shape, bf16),
             pltpu.VMEM((width, features), bf16),
-            dma((nr,)), dma((nr,)), dma((nz,)), dma((nz,)), dma((nz, nr)), dma((nz, nr)), dma((nz, 2)), dma((nz, 2)),
+            dma((nr,)), dma((nr,)), dma((nz,)), dma((nz,)), dma((nz, nr)), dma((nz, nr)), dma((nz, 4)), dma((nz, 4)),
             dma, dma, dma,
         ],
         compiler_params=pltpu.CompilerParams(collective_id=0, has_side_effects=True, vmem_limit_bytes=20 << 20),

time: 51 us -> 50.2 us (0.984)
  Pallas kernels: 50.9 us -> 50.1 us
    pallas_call x1, Pallas kernels: 43.8 us -> 43 us  [gather_and_project(): pl.pallas_call(functools.partial(gather_kernel, nz, ny), out_shape=jax.Sh...]
where the time goes in v6:
time: 50.2 us; the launch traced here: 50.1 us
  Pallas kernels  50.1 us (100%)
    pallas_call x1, Pallas kernels, gather_and_project(): pl.pallas_call(functools.partial(gather_kernel, nz, ny), out_shape=jax.Sh...  43 us
    pallas_call x1, Pallas kernels, attend(): pl.pallas_call(functools.partial(attend_kernel, chunk, nz, ny), out_shape...  7.03 us

profile of v6, /device:TPU:1, one launch (start us, length us, event | category | flops | bytes accessed | tf_op | source)
XLA Modules:
  0.0 50.1 jit_solution(11953742661130853560)
XLA Ops:
  0.0 0.0 copy-start
  0.0 43.0 %shard_map.46.kv = bf16[64,32,2048]{2,1,0:T(8,128)(2,1)S(1)} custom-call(s32[2,32]{1,0:T(2,128)} %bitcast.7, bf16[4,2,16,896]{3,2,1,0:T(8,128)(2,1)} %bitcast.10, bf16[14336,128]{1,0:T(8,128)(2,1)} %bitcast.9), custom_call_target="tpu_custom_call" | custom-call | flops 7516192768 | bytes 16777216 | tf_op jit(solution)/shard_map/pallas_call | solution.py:212
  43.1 0.0 copy-done
  43.1 7.0 %shard_map.47 = bf16[2048,1024]{1,0:T(8,128)(2,1)} custom-call(s32[2,32]{1,0:T(2,128)} %bitcast.8, bf16[2048,1024]{1,0:T(8,128)(2,1)S(1)} %copy-done, bf16[64,32,2048]{2,1,0:T(8,128)(2,1)S(1)} %shard_map.46.kv), custom_call_target="tpu_custom_call" | custom-call | flops 536870912 | bytes 17825792 | tf_op jit(solution)/shard_map/pallas_call | solution.py:289
Async XLA Ops:
  0.0 43.1 %copy-start = (bf16[2048,1024]{1,0:T(8,128)(2,1)S(1)}, bf16[2048,1024]{1,0:T(8,128)(2,1)}, u32[]{:S(2)}) copy-start(bf16[2048,1024]{1,0:T(8,128)(2,1)} %q.1) | copy-start | bytes 12582916
